TPU v7x, 32 devices: a whole 2x2x4 slice. The times are simulated.
32 devices in a mesh: gx: 8 (over y, x, core), gy: 4 (over z).
Axes of the slice: x: 2, y: 2, z: 4, core: 2. Of those that a mesh axis runs over, the one named last changes fastest.
Arguments:
- thinker_normed: bfloat16 [4, 16, 8192], P(None, None, 'gx'), may hold values from -6 to 6
- thinker_resid: bfloat16 [4, 16, 8192], P('gy', None, 'gx'), may hold values from -6 to 6
- gate_weight: bfloat16 [8192, 29568], P('gx', 'gy'), may hold values from -0.0625 to 0.0625
- up_weight: bfloat16 [8192, 29568], P('gx', 'gy'), may hold values from -0.0625 to 0.0625
- down_weight: bfloat16 [29568, 8192], P('gy', 'gx'), may hold values from -0.03125 to 0.03125
- bridge_weight: bfloat16 [8192, 3584], P('gx'), may hold values from -0.0625 to 0.0625
- talker_stream: bfloat16 [4, 1536, 3584], P('gy', 'gx'), may hold values from -6 to 6
- norm_gain: float32 [3584], replicated, may hold values from 0.5 to 2
- w_query: bfloat16 [3584, 1792], P(None, 'gy'), may hold values from -0.09375 to 0.09375
- w_key: bfloat16 [3584, 256], P(None, 'gy'), may hold values from -0.09375 to 0.09375
- w_value: bfloat16 [3584, 256], P(None, 'gy'), may hold values from -0.09375 to 0.09375
- a_query: bfloat16 [3584, 64], replicated, may hold values from -0.09375 to 0.09375
- b_query: bfloat16 [64, 1792], replicated, may hold values from -0.75 to 0.75
- a_value: bfloat16 [3584, 64], replicated, may hold values from -0.09375 to 0.09375
- b_value: bfloat16 [64, 256], replicated, may hold values from -0.75 to 0.75
- text_index: int32 [4, 1536], P('gy', 'gx'), may hold values from 0 to 15
- span_offset: int32 [4], P('gy'), may hold values from 1 to 1535
- out_grad: bfloat16 [4, 1536, 1792], P('gy', 'gx'), may hold values from -6 to 6
Outputs:
- attn_out: bfloat16 [4, 1536, 1792], P('gy', 'gx')
- grad_aq: float32 [3584, 64], replicated
- grad_bq: float32 [64, 1792], replicated
- grad_av: float32 [3584, 64], replicated
- grad_bv: float32 [64, 256], replicated
All inputs are finite; a program needn't handle non-finite values.
Results may differ from a plain program's by a relative error of at most 0.035.
Values may be sent and summed in bfloat16 or wider, within the bound.
No kernel may reach another device: no remote copies, remote signals or barrier semaphores. Data moves between devices by JAX's collectives and lax.ppermute only.
A program may use at most 192 MiB of HBM per device.

v0:
```python
import math
import jax
import jax.numpy as jnp
from jax import lax
from jax.sharding import PartitionSpec as P

HEADS = 14
KVH = 2
HD = 128
rope_base = 1000000.0
norm_eps = 1e-06


def angle_tables(first_pos, length):
    position = (first_pos + jnp.arange(length, dtype=jnp.int32)).astype(jnp.float32)
    frequency = rope_base ** (-(2.0 * jnp.arange(HD // 2, dtype=jnp.float32)) / HD)
    angles = position[:, None] * frequency[None, :]
    return (jnp.cos(angles), jnp.sin(angles))


def rotate(tensor, cosine, sine_table, signed):
    layout = (cosine.shape[0],) + (1,) * (tensor.ndim - 2) + (cosine.shape[1],)
    cosine = cosine.reshape(layout)
    sine_part = sine_table.reshape(layout) * signed
    half_width = tensor.shape[-1] // 2
    first_half = tensor[..., :half_width]
    second_half = tensor[..., half_width:]
    return jnp.concatenate(
        [
            first_half * cosine - second_half * sine_part,
            second_half * cosine + first_half * sine_part,
        ],
        axis=-1,
    )


def on_device(
    thinker_normed,
    thinker_resid,
    gate_weight,
    up_weight,
    down_weight,
    bridge_weight,
    talker_stream,
    norm_gain,
    w_query,
    w_key,
    w_value,
    a_query,
    b_query,
    a_value,
    b_value,
    text_index,
    span_offset,
    out_grad,
):
    seq_count, rows_seq, columns = thinker_normed.shape
    normed = thinker_normed.reshape(seq_count * rows_seq, columns)
    ff_local = gate_weight.shape[1]
    block = normed
    gate_part = jnp.dot(block, gate_weight, preferred_element_type=jnp.float32)
    up_part = jnp.dot(block, up_weight, preferred_element_type=jnp.float32)
    both_parts = lax.psum_scatter(
        jnp.concatenate([gate_part, up_part], axis=1), "gx", scatter_dimension=0, tiled=True
    )
    hidden = (jax.nn.silu(both_parts[:, :ff_local]) * both_parts[:, ff_local:]).astype(jnp.bfloat16)
    partial_out = jnp.dot(
        lax.all_gather(hidden, "gx", axis=0, tiled=True),
        down_weight,
        preferred_element_type=jnp.float32,
    )
    summed = lax.psum_scatter(partial_out, "gy", scatter_dimension=0, tiled=True)
    thinker_out = (summed + thinker_resid[0].astype(jnp.float32)).astype(jnp.bfloat16)
    bridge_part = jnp.dot(thinker_out, bridge_weight, preferred_element_type=jnp.float32)
    bridge = lax.psum(bridge_part, "gx").astype(jnp.bfloat16)
    tokens = talker_stream.shape[1]
    groups = HEADS // KVH
    scale = 1.0 / math.sqrt(HD)
    picks = (text_index[0][:, None] == jnp.arange(rows_seq, dtype=jnp.int32)[None, :]).astype(
        jnp.bfloat16
    )
    mixed = talker_stream[0].astype(jnp.float32) + jnp.dot(
        picks, bridge, preferred_element_type=jnp.float32
    )
    normal = (
        mixed * lax.rsqrt(jnp.mean(mixed * mixed, axis=1, keepdims=True) + norm_eps) * norm_gain
    ).astype(jnp.bfloat16)
    low_query = jnp.dot(normal, a_query, preferred_element_type=jnp.float32).astype(jnp.bfloat16)
    low_value = jnp.dot(normal, a_value, preferred_element_type=jnp.float32).astype(jnp.bfloat16)
    slab_rows = lax.all_gather(normal, "gy", axis=0, tiled=True)
    projected = jnp.concatenate(
        [
            jnp.dot(slab_rows, w_query, preferred_element_type=jnp.float32),
            jnp.dot(slab_rows, w_key, preferred_element_type=jnp.float32),
            jnp.dot(slab_rows, w_value, preferred_element_type=jnp.float32),
        ],
        axis=1,
    )
    returned = lax.all_to_all(projected, "gy", split_axis=0, concat_axis=1, tiled=True)
    parcels = returned.reshape(tokens, lax.axis_size("gy"), -1)
    query_cols = w_query.shape[1]
    key_cols = w_key.shape[1]
    base_query = parcels[:, :, :query_cols].reshape(tokens, -1)
    base_key = parcels[:, :, query_cols : query_cols + key_cols].reshape(tokens, -1)
    base_value = parcels[:, :, query_cols + key_cols :].reshape(tokens, -1)
    first_pos = lax.axis_index("gx") * tokens
    cosine, sine_table = angle_tables(first_pos, tokens)
    query_pre = base_query + jnp.dot(low_query, b_query, preferred_element_type=jnp.float32)
    query = rotate(query_pre.reshape(tokens, KVH, groups, HD), cosine, sine_table, 1.0).astype(
        jnp.bfloat16
    )
    key_local = (
        rotate(base_key.reshape(tokens, KVH, HD), cosine, sine_table, 1.0)
        .astype(jnp.bfloat16)
        .reshape(tokens, KVH * HD)
    )
    value_local = (
        base_value + jnp.dot(low_value, b_value, preferred_element_type=jnp.float32)
    ).astype(jnp.bfloat16)
    key_all, value_all = (
        lax.all_gather(key_local, "gx", axis=0, tiled=True),
        lax.all_gather(value_local, "gx", axis=0, tiled=True),
    )
    length = key_all.shape[0]
    key_rows = key_all.reshape(length, KVH, HD)
    value_rows = value_all.reshape(length, KVH, HD)
    query_places = first_pos + jnp.arange(tokens, dtype=jnp.int32)
    key_places = jnp.arange(length, dtype=jnp.int32)
    causal = (key_places[None, :] <= query_places[:, None]) | (key_places[None, :] < span_offset[0])
    scores = (
        jnp.einsum("tkgd,skd->kgts", query, key_rows, preferred_element_type=jnp.float32) * scale
    )
    scores = jnp.where(causal, scores, -1e30)
    row_max = jnp.max(scores, axis=-1, keepdims=True)
    weights = jnp.exp(scores - row_max)
    probs = (weights / jnp.sum(weights, axis=-1, keepdims=True)).astype(jnp.bfloat16)
    attended = jnp.einsum(
        "kgts,skd->tkgd", probs, value_rows, preferred_element_type=jnp.float32
    ).astype(jnp.bfloat16)
    grad_four = out_grad[0].reshape(tokens, KVH, groups, HD)
    inner_prod = jnp.sum(grad_four.astype(jnp.float32) * attended.astype(jnp.float32), axis=-1)
    dprob = jnp.einsum("tkgd,skd->kgts", grad_four, value_rows, preferred_element_type=jnp.float32)
    dscore = (
        probs.astype(jnp.float32) * (dprob - jnp.transpose(inner_prod, (1, 2, 0))[..., None])
    ).astype(jnp.bfloat16)
    dquery = (
        jnp.einsum("kgts,skd->tkgd", dscore, key_rows, preferred_element_type=jnp.float32) * scale
    )
    query_grad = (
        rotate(dquery, cosine, sine_table, -1.0).reshape(tokens, HEADS * HD).astype(jnp.bfloat16)
    )
    block = probs
    term = jnp.einsum("kgts,tkgd->skd", block, grad_four, preferred_element_type=jnp.float32)
    value_grad = lax.psum_scatter(
        term.reshape(lax.axis_size("gx") * tokens, KVH * HD), "gx", scatter_dimension=0, tiled=True
    ).astype(jnp.bfloat16)
    part_bq = jnp.einsum("tr,tc->rc", low_query, query_grad, preferred_element_type=jnp.float32)
    part_bv = jnp.einsum("tr,tc->rc", low_value, value_grad, preferred_element_type=jnp.float32)
    dlow_query = jnp.einsum(
        "tc,rc->tr", query_grad, b_query, preferred_element_type=jnp.float32
    ).astype(jnp.bfloat16)
    dlow_value = jnp.einsum(
        "tc,rc->tr", value_grad, b_value, preferred_element_type=jnp.float32
    ).astype(jnp.bfloat16)
    part_aq = jnp.einsum("td,tr->dr", normal, dlow_query, preferred_element_type=jnp.float32)
    part_av = jnp.einsum("td,tr->dr", normal, dlow_value, preferred_element_type=jnp.float32)
    grad_aq, grad_bq, grad_av, grad_bv = lax.psum(
        (part_aq, part_bq, part_av, part_bv), ("gx", "gy")
    )
    attn_out = attended.reshape(1, tokens, HEADS * HD)
    return (attn_out, grad_aq, grad_bq, grad_av, grad_bv)


def solution(mesh):
    return jax.shard_map(
        on_device,
        mesh=mesh,
        in_specs=(
            P(None, None, "gx"),
            P("gy", None, "gx"),
            P("gx", "gy"),
            P("gx", "gy"),
            P("gy", "gx"),
            P("gx", None),
            P("gy", "gx", None),
            P(),
            P(None, "gy"),
            P(None, "gy"),
            P(None, "gy"),
            P(),
            P(),
            P(),
            P(),
            P("gy", "gx"),
            P("gy"),
            P("gy", "gx", None),
        ),
        out_specs=(P("gy", "gx", None), P(), P(), P(), P()),
        check_vma=False,
    )
```

profile of v0, /device:TPU:0, one launch (start us, length us, event | category | flops | bytes accessed | tf_op | source)
XLA Modules:
  0.0 564.3 jit_solution(9775176805287978987)
XLA Ops:
  7.2 10.2 %fusion.54 = f32[64,7392]{1,0:T(8,128)S(1)} fusion(bf16[64,1024]{1,0:T(8,128)(2,1)} %bitcast.100, bf16[1024,7392]{0,1:T(8,128)(2,1)} %param.20), kind=kOutput, calls=%fused_computation.78 | convolution fusion | flops 968884224 | bytes 17162240 | tf_op jit(solution)/shard_map/dot_general | solution.py:61
  17.4 10.0 %fusion.55 = f32[64,7392]{1,0:T(8,128)S(1)} fusion(bf16[64,1024]{1,0:T(8,128)(2,1)S(1)} %bitcast.101, bf16[1024,7392]{0,1:T(8,128)(2,1)} %param.21), kind=kOutput, calls=%fused_computation.79 | convolution fusion | flops 968884224 | bytes 17162240 | tf_op jit(solution)/shard_map/dot_general | solution.py:62
  27.4 2.5 pad_maximum_fusion
  29.9 52.0 %reduce-scatter.6.cloned.1.call-done = f32[8,14784]{1,0:T(8,128)} async-done(((f32[64,14784]{1,0:T(8,128)}), f32[8,14784]{1,0:T(8,128)}) %reduce-scatter.6.cloned.1.call-update) | async-done | bytes 473104 | tf_op jit(solution)/shard_map/reduce_scatter | solution.py:63
  81.9 1.2 fusion.32
  83.1 10.8 %all_gather.12 = bf16[64,7392]{1,0:T(8,128)(2,1)S(1)} all-gather(bf16[8,7392]{1,0:T(8,128)(2,1)S(1)} %fusion.32), channel_id=1, replica_groups=mesh['gx'=8,'gy'=4] {'gx'}, dimensions={0}, use_global_device_ids=true | all-gather | bytes 1064448 | tf_op jit(solution)/shard_map/all_gather | solution.py:68
  93.9 8.8 %fusion.56 = f32[64,1024]{1,0:T(8,128)} fusion(bf16[64,7392]{1,0:T(8,128)(2,1)S(1)} %all_gather.12, bf16[7392,1024]{1,0:T(8,128)(2,1)} %param.22), kind=kOutput, calls=%fused_computation.80 | convolution fusion | flops 968884224 | bytes 16347136 | tf_op jit(solution)/shard_map/dot_general | solution.py:67
  102.7 20.1 %reduce-scatter.8.cloned.1.call-done = f32[16,1024]{1,0:T(8,128)} async-done(((f32[64,1024]{1,0:T(8,128)}), f32[16,1024]{1,0:T(8,128)}) %reduce-scatter.8.cloned.1.call-update) | async-done | bytes 65552 | tf_op jit(solution)/shard_map/reduce_scatter | solution.py:72
  122.8 4.2 fusion.41
  127.0 25.4 %all-reduce.5 = bf16[16,3584]{1,0:T(8,128)(2,1)S(1)} all-reduce(f32[16,3584]{1,0:T(8,128)S(1)} %fusion.41), channel_id=1, replica_groups=mesh['gx'=8,'gy'=4] {'gx'}, use_global_device_ids=true, to_apply=%region_2.3 | all-reduce | flops 57344 | bytes 344064 | tf_op jit(solution)/shard_map/psum | solution.py:75
  152.4 2.0 multiply_reduce_fusion
  154.4 1.5 multiply_convert_fusion
  155.9 99.9 %all-gather.2.cloned.1.call-done = bf16[768,3584]{1,0:T(8,128)(2,1)} async-done(((bf16[192,3584]{1,0:T(8,128)(2,1)}), bf16[768,3584]{1,0:T(8,128)(2,1)}) %all-gather.2.cloned.1.call-update) | async-done | bytes 5505040 | tf_op jit(solution)/shard_map/all_gather | solution.py:90
  255.8 5.4 fusion.57
  261.2 1.8 fusion.58
  263.0 1.8 fusion.59
  264.9 1.8 copy.44
  266.7 4.6 all-to-all-start
  273.9 1.7 reshape_squeeze.3
  277.1 1.6 convolution_convert_fusion.4
  278.7 38.4 %all-to-all-done = f32[4,192,576]{2,1,0:T(8,128)} async-done(((f32[4,192,576]{2,1,0:T(8,128)}), f32[4,192,576]{2,1,0:T(8,128)}, u32[]{:S(2)}, u32[]{:S(2)}) %all-to-all-start) | async-done | bytes 1769504 | tf_op jit(solution)/shard_map/all_to_all | solution.py:99
  317.0 1.5 slice.50
  318.6 2.1 fusion.51
  320.7 2.2 copy.52
  322.8 2.5 reshape.208
  325.3 1.5 convolution_add_fusion.1
  326.8 1.7 reshape.209
  328.4 2.1 fusion.52
  330.6 1.2 copy.47
  332.9 11.6 %all_gather.15 = bf16[1536,256]{1,0:T(8,128)(2,1)} all-gather(bf16[192,256]{1,0:T(8,128)(2,1)S(1)} %copy.50), channel_id=1, replica_groups=mesh['gx'=8,'gy'=4] {'gx'}, dimensions={0}, use_global_device_ids=true | all-gather | bytes 884736 | tf_op jit(solution)/shard_map/all_gather | solution.py:121
  344.5 2.3 copy.51
  346.8 3.4 subtract_convert_fusion.1
  350.2 10.5 %fusion.53 = (f32[2,7,192]{2,1,0:T(8,128)S(1)}, f32[2,7,192,1536]{3,2,1,0:T(8,128)}) fusion(pred[192,1536]{1,0:T(8,128)(4,1)S(1)} %copy-done.19, bf16[1536,2,128,1]{0,2,3,1:T(8,128)(2,1)} %bitcast.104, bf16[192,2,7,64]{3,0,2,1:T(8,128)(2,1)} %get-tuple-element.10, bf16[192,2,7,64]{3,0,2,1:T(8,128)(2,1)} %get-tuple-element.9), kind=kOutput, calls=%fused_computation.77 | convolution fusion | flops 1074857472 | bytes 18295296 | tf_op jit(solution)/shard_map/sub | solution.py:135
  360.8 7.1 %divide_convert_fusion = bf16[2,7,192,1536]{3,2,1,0:T(8,128)(2,1)S(1)} fusion(f32[2,7,192,1536]{3,2,1,0:T(8,128)} %get-tuple-element.25, f32[2,7,192]{2,1,0:T(8,128)S(1)} %get-tuple-element.24), kind=kLoop, calls=%fused_computation.5 | loop fusion | flops 8257536 | bytes 24783360 | tf_op jit(solution)/shard_map/convert_element_type | solution.py:136
  367.9 1.5 fusion.28
  369.4 1.7 copy-done.2
  371.1 1.7 copy.77
  372.8 1.2 copy.45
  374.4 11.2 %all_gather.14 = bf16[1536,256]{1,0:T(8,128)(2,1)} all-gather(bf16[192,256]{1,0:T(8,128)(2,1)S(1)} %fusion.22), channel_id=1, replica_groups=mesh['gx'=8,'gy'=4] {'gx'}, dimensions={0}, use_global_device_ids=true | all-gather | bytes 884736 | tf_op jit(solution)/shard_map/all_gather | solution.py:122
  385.7 2.2 reshape.206
  387.9 6.6 %multiply_reduce_fusion.1 = (f32[192,2,7]{0,2,1:T(8,128)S(1)}, bf16[192,2,7,128]{3,0,2,1:T(8,128)(2,1)}) fusion(bf16[192,2,7,128]{3,2,1,0:T(8,128)(2,1)S(1)} %copy-done.7, bf16[2,7,192,1536]{3,2,1,0:T(8,128)(2,1)} %copy-done.2, bf16[1536,2,128,1]{2,1,0,3:T(2,128)(2,1)S(1)} %bitcast.98), kind=kOutput, calls=%fused_computation.25 | convolution fusion | flops 1058682240 | bytes 10430976 | tf_op jit(solution)/shard_map/kgts,skd->tkgd/dot_general | solution.py:137
  394.6 9.5 %fusion.17 = f32[192,2,7,128]{3,0,2,1:T(8,128)} fusion(bf16[1536,2,128,1]{0,2,3,1:T(8,128)(2,1)} %bitcast.105, bf16[2,7,192,1536]{3,2,1,0:T(8,128)(2,1)} %copy-done.2, f32[2,7,192]{2,1,0:T(8,128)S(1)} %bitcast.107, bf16[1536,2,128,1]{2,1,0,3:T(2,128)(2,1)S(1)} %bitcast.99, bf16[192,2,7,128]{3,2,1,0:T(8,128)(2,1)S(1)} %copy-done.7), kind=kOutput, calls=%fused_computation.22 | convolution fusion | flops 2130788352 | bytes 11905536 | tf_op jit(solution)/shard_map/kgts,skd->tkgd/dot_general | solution.py:147
  404.0 2.3 subtract_convert_fusion
  409.0 1.9 fusion.23
  412.8 1.4 fusion.24
  414.7 1.6 reshape.210
  416.3 136.6 %all-reduce.4.cloned.1.call-done = (f32[3584,64]{0,1:T(8,128)}, f32[64,1792]{1,0:T(8,128)}, f32[3584,64]{0,1:T(8,128)}, f32[64,256]{1,0:T(8,128)}) async-done(((f32[3584,64]{0,1:T(8,128)}, f32[64,1792]{1,0:T(8,128)}, f32[3584,64]{0,1:T(8,128)}, f32[64,256]{1,0:T(8,128)}), (f32[3584,64]{0,1:T(8,128)}, f32[64,1792]{1,0:T(8,128)}, f32[3584,64]{0,1:T(8,128)}, f32[64,256]{1,0:T(8,128)})) %all-reduce.4.cloned.1.call-update) | async-done | bytes 2359312 | tf_op jit(solution)/shard_map/psum | solution.py:167
  552.9 2.3 copy.105
  (84 shorter events, 12.6 us)
Async XLA Ops:
  7.2 248.6 %copy-start = (bf16[3584,448]{0,1:T(8,128)(2,1)S(1)}, bf16[3584,448]{0,1:T(8,128)(2,1)}, u32[]{:S(2)}) copy-start(bf16[3584,448]{0,1:T(8,128)(2,1)} %param.26) | copy-start | bytes 9633796
  7.2 74.7 %reduce-scatter.6.cloned.1.call-start = ((), (), s32[]{:S(2)}) async-start(), calls=%async_computation.4 | async-start | bytes 4276224 | tf_op jit(solution)/shard_map/reduce_scatter | solution.py:63
  7.2 10.2 %copy-start.9 = (bf16[4,16,1024]{2,1,0:T(8,128)(2,1)S(1)}, bf16[4,16,1024]{2,1,0:T(8,128)(2,1)}, u32[]{:S(2)}) copy-start(bf16[4,16,1024]{2,1,0:T(8,128)(2,1)} %param.18) | copy-start | bytes 393220
  29.9 92.9 %reduce-scatter.8.cloned.1.call-start = ((), (), s32[]{:S(2)}) async-start(), calls=%async_computation.5 | async-start | bytes 327680 | tf_op jit(solution)/shard_map/reduce_scatter | solution.py:72
  93.9 29.0 %copy-start.22 = (bf16[1,16,1024]{2,1,0:T(8,128)(2,1)S(1)}, bf16[1,16,1024]{2,1,0:T(8,128)(2,1)}, u32[]{:S(2)}) copy-start(bf16[1,16,1024]{2,1,0:T(8,128)(2,1)} %param.19) | copy-start | bytes 98308
  102.7 153.1 %all-gather.2.cloned.1.call-start = ((), (), s32[]{:S(2)}) async-start(), calls=%async_computation.6 | async-start | bytes 6881280 | tf_op jit(solution)/shard_map/all_gather | solution.py:90
  152.4 2.0 copy-start.23
  255.8 5.4 copy-start.4
  255.8 5.4 copy-start.14
  261.2 1.8 copy-start.15
  266.7 7.2 %copy-start.13 = (bf16[1,192,1792]{2,1,0:T(8,128)(2,1)S(1)}, bf16[1,192,1792]{2,1,0:T(8,128)(2,1)}, u32[]{:S(2)}) copy-start(bf16[1,192,1792]{2,1,0:T(8,128)(2,1)} %param.35) | copy-start | bytes 2064388
  266.7 50.3 %all-to-all-start = ((f32[4,192,576]{2,1,0:T(8,128)}), f32[4,192,576]{2,1,0:T(8,128)}, u32[]{:S(2)}, u32[]{:S(2)}) async-start(f32[4,192,576]{2,1,0:T(8,128)} %bitcast.4), calls=%async_computation.2 | async-start | bytes 3932160 | tf_op jit(solution)/shard_map/all_to_all | solution.py:99
  271.2 5.3 copy-start.3
  271.3 5.3 copy-start.16
  271.3 139.6 %reduce-scatter.10.cloned.1.call-start = ((), (), s32[]{:S(2)}) async-start(), calls=%async_computation.7 | async-start | bytes 1769472
  322.8 2.5 copy-start.10
  331.8 15.0 %copy-start.5 = (f32[192,2,7,64]{3,2,1,0:T(8,128)S(1)}, f32[192,2,7,64]{3,2,1,0:T(8,128)}, u32[]{:S(2)}) copy-start(f32[192,2,7,64]{3,2,1,0:T(8,128)} %get-tuple-element.15) | copy-start | bytes 2064388
  346.8 3.4 copy-start.19
  360.8 7.1 %copy-start.6 = (bf16[192,2,7,128]{3,2,1,0:T(8,128)(2,1)S(1)}, bf16[192,2,7,128]{3,2,1,0:T(8,128)(2,1)}, u32[]{:S(2)}) copy-start(bf16[192,2,7,128]{3,2,1,0:T(8,128)(2,1)} %reshape_squeeze.3) | copy-start | bytes 2064388
  367.9 3.2 copy-start.2
  372.7 1.5 copy-start.20
  372.8 180.1 %all-reduce.4.cloned.1.call-start = ((), (), s32[]{:S(2)}) async-start(), calls=%async_computation.8 | async-start | bytes 4718592 | tf_op jit(solution)/shard_map/psum | solution.py:167
  372.8 15.1 %copy-start.7 = (bf16[192,2,7,128]{3,2,1,0:T(8,128)(2,1)S(1)}, bf16[192,2,7,128]{3,2,1,0:T(8,128)(2,1)}, u32[]{:S(2)}) copy-start(bf16[192,2,7,128]{3,2,1,0:T(8,128)(2,1)} %reshape_squeeze.3) | copy-start | bytes 2064388
  394.6 9.5 %copy-start.18 = (f32[192,64]{1,0:T(8,128)S(1)}, f32[192,64]{1,0:T(8,128)}, u32[]{:S(2)}) copy-start(f32[192,64]{1,0:T(8,128)} %get-tuple-element.19) | copy-start | bytes 147460
  406.8 2.3 copy-start.11
  412.8 1.5 copy-start.8
  552.9 2.3 copy-start.17
  552.9 3.1 copy-start.12
  552.9 4.0 copy-start.21
  552.9 4.7 copy-start.1
Sparse Core Ops, SparseCore 0:
  30.0 51.8 reduce-scatter.5
  102.8 19.9 reduce-scatter.7
  156.0 99.6 all-gather.1
  372.9 36.5 reduce-scatter.9
  415.9 136.9 all-reduce.3
where the time goes:
time: 573 us; the launch traced here: 564 us
  waiting for transfers between devices  347 us (61%)
  matrix products  81.1 us (14%)
  blocking collectives  59 us (10%)
  local copies, waits for them, and re-layouts  35.9 us (6%)
  other arithmetic  21.5 us (4%)
  between operations  15.1 us (3%)
    psum x1, waiting for transfers between devices, on_device(): lax.psum((part_aq, part_bq, part_av, part_bv), ('gx', 'gy'))  137 us
    all_gather x1, waiting for transfers between devices, on_device(): slab_rows = lax.all_gather(normal, 'gy', axis=0, tiled=True)  99.9 us
    reduce_scatter x1, waiting for transfers between devices, on_device(): lax.psum_scatter(jnp.concatenate([gate_part, up_part], axis=1), 'gx', sca...  52 us
    all_to_all x1, waiting for transfers between devices, on_device(): lax.all_to_all(projected, 'gy', split_axis=0, concat_axis=1, tiled=True)  38.4 us
    psum x1, blocking collectives, on_device(): bridge = lax.psum(bridge_part, 'gx').astype(jnp.bfloat16)  25.4 us
    reduce_scatter x1, waiting for transfers between devices, on_device(): lax.psum_scatter(partial_out, 'gy', scatter_dimension=0, tiled=True)  20.1 us
    all_gather x1, blocking collectives, on_device(): lax.all_gather(key_local, 'gx', axis=0, tiled=True)  11.6 us
  transfers between devices with their start and end apart: 6, of which 5 were waited for; matrix products, arithmetic and copies ran while one was open for 6% of the time, Pallas kernels for 0%

commit v1 on v0

--- a/solution.py
+++ b/solution.py
@@ -165,7 +165,7 @@
     part_aq = jnp.einsum("td,tr->dr", normal, dlow_query, preferred_element_type=jnp.float32)
     part_av = jnp.einsum("td,tr->dr", normal, dlow_value, preferred_element_type=jnp.float32)
     grad_aq, grad_bq, grad_av, grad_bv = lax.psum(
-        (part_aq, part_bq, part_av, part_bv), ("gx", "gy")
+        lax.psum((part_aq, part_bq, part_av, part_bv), axis_name="gy"), axis_name="gx"
     )
     attn_out = attended.reshape(1, tokens, HEADS * HD)
     return (attn_out, grad_aq, grad_bq, grad_av, grad_bv)

time: 573 us -> 594 us (1.037)
  waiting for transfers between devices: 347 us -> 367 us
    psum x1 -> x2, waiting for transfers between devices: 137 us -> 157 us  [the longest x1 93.3 us: on_device(): lax.psum((part_aq, part_bq, part_av, part_bv), axis_name='gy')]
  transfers between devices with their start and end apart: 6 -> 7, of which waited for: 5 -> 6; matrix products, arithmetic and copies ran while one was open for 6% -> 6% of each run, Pallas kernels for 0% -> 0%
where the time goes in v1:
time: 594 us; the launch traced here: 585 us
  waiting for transfers between devices  367 us (62%)
  matrix products  81.1 us (14%)
  blocking collectives  59.2 us (10%)
  local copies, waits for them, and re-layouts  35.7 us (6%)
  other arithmetic  21.5 us (4%)
  between operations  15.4 us (3%)
    all_gather x1, waiting for transfers between devices, on_device(): slab_rows = lax.all_gather(normal, 'gy', axis=0, tiled=True)  99.9 us
    psum x1, waiting for transfers between devices, on_device(): lax.psum((part_aq, part_bq, part_av, part_bv), axis_name='gy')  93.3 us
    psum x1, waiting for transfers between devices, on_device(): lax.psum(lax.psum((part_aq, part_bq, part_av, part_bv), axis_name='gy'),...  63.8 us
    reduce_scatter x1, waiting for transfers between devices, on_device(): lax.psum_scatter(jnp.concatenate([gate_part, up_part], axis=1), 'gx', sca...  52 us
    all_to_all x1, waiting for transfers between devices, on_device(): lax.all_to_all(projected, 'gy', split_axis=0, concat_axis=1, tiled=True)  38.4 us
    psum x1, blocking collectives, on_device(): bridge = lax.psum(bridge_part, 'gx').astype(jnp.bfloat16)  25.4 us
    reduce_scatter x1, waiting for transfers between devices, on_device(): lax.psum_scatter(partial_out, 'gy', scatter_dimension=0, tiled=True)  20.1 us
  transfers between devices with their start and end apart: 7, of which 6 were waited for; matrix products, arithmetic and copies ran while one was open for 6% of the time, Pallas kernels for 0%

profile of v1, /device:TPU:0, one launch (start us, length us, event | category | flops | bytes accessed | tf_op | source)
XLA Modules:
  0.0 585.3 jit_solution(6433655267056165756)
XLA Ops:
  7.2 10.2 %fusion.54 = f32[64,7392]{1,0:T(8,128)S(1)} fusion(bf16[64,1024]{1,0:T(8,128)(2,1)} %bitcast.100, bf16[1024,7392]{0,1:T(8,128)(2,1)} %param.20), kind=kOutput, calls=%fused_computation.78 | convolution fusion | flops 968884224 | bytes 17162240 | tf_op jit(solution)/shard_map/dot_general | solution.py:61
  17.4 10.0 %fusion.55 = f32[64,7392]{1,0:T(8,128)S(1)} fusion(bf16[64,1024]{1,0:T(8,128)(2,1)S(1)} %bitcast.101, bf16[1024,7392]{0,1:T(8,128)(2,1)} %param.21), kind=kOutput, calls=%fused_computation.79 | convolution fusion | flops 968884224 | bytes 17162240 | tf_op jit(solution)/shard_map/dot_general | solution.py:62
  27.4 2.5 pad_maximum_fusion
  30.0 52.0 %reduce-scatter.6.cloned.1.call-done = f32[8,14784]{1,0:T(8,128)} async-done(((f32[64,14784]{1,0:T(8,128)}), f32[8,14784]{1,0:T(8,128)}) %reduce-scatter.6.cloned.1.call-update) | async-done | bytes 473104 | tf_op jit(solution)/shard_map/reduce_scatter | solution.py:63
  81.9 1.2 fusion.32
  83.1 10.8 %all_gather.12 = bf16[64,7392]{1,0:T(8,128)(2,1)S(1)} all-gather(bf16[8,7392]{1,0:T(8,128)(2,1)S(1)} %fusion.32), channel_id=1, replica_groups=mesh['gx'=8,'gy'=4] {'gx'}, dimensions={0}, use_global_device_ids=true | all-gather | bytes 1064448 | tf_op jit(solution)/shard_map/all_gather | solution.py:68
  93.9 8.8 %fusion.56 = f32[64,1024]{1,0:T(8,128)} fusion(bf16[64,7392]{1,0:T(8,128)(2,1)S(1)} %all_gather.12, bf16[7392,1024]{1,0:T(8,128)(2,1)} %param.22), kind=kOutput, calls=%fused_computation.80 | convolution fusion | flops 968884224 | bytes 16347136 | tf_op jit(solution)/shard_map/dot_general | solution.py:67
  102.8 20.1 %reduce-scatter.8.cloned.1.call-done = f32[16,1024]{1,0:T(8,128)} async-done(((f32[64,1024]{1,0:T(8,128)}), f32[16,1024]{1,0:T(8,128)}) %reduce-scatter.8.cloned.1.call-update) | async-done | bytes 65552 | tf_op jit(solution)/shard_map/reduce_scatter | solution.py:72
  122.8 4.2 fusion.41
  127.0 25.4 %all-reduce.9 = bf16[16,3584]{1,0:T(8,128)(2,1)S(1)} all-reduce(f32[16,3584]{1,0:T(8,128)S(1)} %fusion.41), channel_id=1, replica_groups=mesh['gx'=8,'gy'=4] {'gx'}, use_global_device_ids=true, to_apply=%region_2.3 | all-reduce | flops 57344 | bytes 344064 | tf_op jit(solution)/shard_map/psum | solution.py:75
  152.4 2.0 multiply_reduce_fusion
  154.5 1.5 multiply_convert_fusion
  155.9 99.9 %all-gather.2.cloned.1.call-done = bf16[768,3584]{1,0:T(8,128)(2,1)} async-done(((bf16[192,3584]{1,0:T(8,128)(2,1)}), bf16[768,3584]{1,0:T(8,128)(2,1)}) %all-gather.2.cloned.1.call-update) | async-done | bytes 5505040 | tf_op jit(solution)/shard_map/all_gather | solution.py:90
  255.8 5.4 fusion.57
  261.2 1.8 fusion.58
  263.0 1.8 fusion.59
  264.9 1.8 copy.44
  266.7 4.6 all-to-all-start
  273.9 1.7 reshape_squeeze.3
  277.1 1.6 convolution_convert_fusion.4
  278.7 38.4 %all-to-all-done = f32[4,192,576]{2,1,0:T(8,128)} async-done(((f32[4,192,576]{2,1,0:T(8,128)}), f32[4,192,576]{2,1,0:T(8,128)}, u32[]{:S(2)}, u32[]{:S(2)}) %all-to-all-start) | async-done | bytes 1769504 | tf_op jit(solution)/shard_map/all_to_all | solution.py:99
  317.0 1.5 slice.50
  318.6 2.1 fusion.51
  320.7 2.2 copy.52
  322.9 2.5 reshape.208
  325.3 1.5 convolution_add_fusion.1
  326.8 1.7 reshape.209
  328.5 2.2 fusion.52
  333.0 11.6 %all_gather.15 = bf16[1536,256]{1,0:T(8,128)(2,1)} all-gather(bf16[192,256]{1,0:T(8,128)(2,1)S(1)} %copy.50), channel_id=1, replica_groups=mesh['gx'=8,'gy'=4] {'gx'}, dimensions={0}, use_global_device_ids=true | all-gather | bytes 884736 | tf_op jit(solution)/shard_map/all_gather | solution.py:121
  344.6 2.3 copy.51
  346.9 3.4 subtract_convert_fusion.1
  350.3 10.6 %fusion.53 = (f32[2,7,192]{2,1,0:T(8,128)S(1)}, f32[2,7,192,1536]{3,2,1,0:T(8,128)}) fusion(pred[192,1536]{1,0:T(8,128)(4,1)S(1)} %copy-done.19, bf16[1536,2,128,1]{0,2,3,1:T(8,128)(2,1)} %bitcast.104, bf16[192,2,7,64]{3,0,2,1:T(8,128)(2,1)} %get-tuple-element.14, bf16[192,2,7,64]{3,0,2,1:T(8,128)(2,1)} %get-tuple-element.13), kind=kOutput, calls=%fused_computation.77 | convolution fusion | flops 1074857472 | bytes 18295296 | tf_op jit(solution)/shard_map/sub | solution.py:135
  360.9 7.1 %divide_convert_fusion = bf16[2,7,192,1536]{3,2,1,0:T(8,128)(2,1)S(1)} fusion(f32[2,7,192,1536]{3,2,1,0:T(8,128)} %get-tuple-element.29, f32[2,7,192]{2,1,0:T(8,128)S(1)} %get-tuple-element.28), kind=kLoop, calls=%fused_computation.5 | loop fusion | flops 8257536 | bytes 24783360 | tf_op jit(solution)/shard_map/convert_element_type | solution.py:136
  367.9 1.5 fusion.28
  369.4 1.7 copy-done.2
  371.1 1.7 copy.77
  372.9 1.2 copy.45
  374.5 11.5 %all_gather.14 = bf16[1536,256]{1,0:T(8,128)(2,1)} all-gather(bf16[192,256]{1,0:T(8,128)(2,1)S(1)} %fusion.22), channel_id=1, replica_groups=mesh['gx'=8,'gy'=4] {'gx'}, dimensions={0}, use_global_device_ids=true | all-gather | bytes 884736 | tf_op jit(solution)/shard_map/all_gather | solution.py:122
  386.0 2.0 reshape.206
  388.0 6.6 %multiply_reduce_fusion.1 = (f32[192,2,7]{0,2,1:T(8,128)S(1)}, bf16[192,2,7,128]{3,0,2,1:T(8,128)(2,1)}) fusion(bf16[192,2,7,128]{3,2,1,0:T(8,128)(2,1)S(1)} %copy-done.7, bf16[2,7,192,1536]{3,2,1,0:T(8,128)(2,1)} %copy-done.2, bf16[1536,2,128,1]{2,1,0,3:T(2,128)(2,1)S(1)} %bitcast.98), kind=kOutput, calls=%fused_computation.25 | convolution fusion | flops 1058682240 | bytes 10430976 | tf_op jit(solution)/shard_map/kgts,skd->tkgd/dot_general | solution.py:137
  394.7 9.5 %fusion.17 = f32[192,2,7,128]{3,0,2,1:T(8,128)} fusion(bf16[1536,2,128,1]{0,2,3,1:T(8,128)(2,1)} %bitcast.105, bf16[2,7,192,1536]{3,2,1,0:T(8,128)(2,1)} %copy-done.2, f32[2,7,192]{2,1,0:T(8,128)S(1)} %bitcast.107, bf16[1536,2,128,1]{2,1,0,3:T(2,128)(2,1)S(1)} %bitcast.99, bf16[192,2,7,128]{3,2,1,0:T(8,128)(2,1)S(1)} %copy-done.7), kind=kOutput, calls=%fused_computation.22 | convolution fusion | flops 2130788352 | bytes 11905536 | tf_op jit(solution)/shard_map/kgts,skd->tkgd/dot_general | solution.py:147
  404.1 2.3 subtract_convert_fusion
  409.1 1.9 fusion.23
  412.9 1.4 fusion.24
  414.4 93.3 %all-reduce.8.cloned.1.call-done = (f32[3584,64]{0,1:T(8,128)}, f32[64,1792]{1,0:T(8,128)}, f32[3584,64]{0,1:T(8,128)}, f32[64,256]{1,0:T(8,128)}) async-done(((f32[3584,64]{0,1:T(8,128)}, f32[64,1792]{1,0:T(8,128)}, f32[3584,64]{0,1:T(8,128)}, f32[64,256]{1,0:T(8,128)}), (f32[3584,64]{0,1:T(8,128)}, f32[64,1792]{1,0:T(8,128)}, f32[3584,64]{0,1:T(8,128)}, f32[64,256]{1,0:T(8,128)})) %all-reduce.8.cloned.1.call-update) | async-done | bytes 2359312 | tf_op jit(solution)/shard_map/psum | solution.py:168
  508.2 1.6 reshape.210
  509.7 63.8 %all-reduce.6.cloned.1.call-done = (f32[3584,64]{0,1:T(8,128)}, f32[64,1792]{1,0:T(8,128)}, f32[3584,64]{0,1:T(8,128)}, f32[64,256]{1,0:T(8,128)}) async-done(((f32[3584,64]{0,1:T(8,128)}, f32[64,1792]{1,0:T(8,128)}, f32[3584,64]{0,1:T(8,128)}, f32[64,256]{1,0:T(8,128)}), (f32[3584,64]{0,1:T(8,128)}, f32[64,1792]{1,0:T(8,128)}, f32[3584,64]{0,1:T(8,128)}, f32[64,256]{1,0:T(8,128)})) %all-reduce.6.cloned.1.call-update) | async-done | bytes 2359312 | tf_op jit(solution)/shard_map/psum | solution.py:167
  573.6 2.3 copy.109
  (87 shorter events, 13.8 us)
Async XLA Ops:
  7.2 248.6 %copy-start = (bf16[3584,448]{0,1:T(8,128)(2,1)S(1)}, bf16[3584,448]{0,1:T(8,128)(2,1)}, u32[]{:S(2)}) copy-start(bf16[3584,448]{0,1:T(8,128)(2,1)} %param.26) | copy-start | bytes 9633796
  7.2 74.8 %reduce-scatter.6.cloned.1.call-start = ((), (), s32[]{:S(2)}) async-start(), calls=%async_computation.4 | async-start | bytes 4276224 | tf_op jit(solution)/shard_map/reduce_scatter | solution.py:63
  7.2 10.2 %copy-start.9 = (bf16[4,16,1024]{2,1,0:T(8,128)(2,1)S(1)}, bf16[4,16,1024]{2,1,0:T(8,128)(2,1)}, u32[]{:S(2)}) copy-start(bf16[4,16,1024]{2,1,0:T(8,128)(2,1)} %param.18) | copy-start | bytes 393220
  29.9 92.9 %reduce-scatter.8.cloned.1.call-start = ((), (), s32[]{:S(2)}) async-start(), calls=%async_computation.5 | async-start | bytes 327680 | tf_op jit(solution)/shard_map/reduce_scatter | solution.py:72
  93.9 29.0 %copy-start.22 = (bf16[1,16,1024]{2,1,0:T(8,128)(2,1)S(1)}, bf16[1,16,1024]{2,1,0:T(8,128)(2,1)}, u32[]{:S(2)}) copy-start(bf16[1,16,1024]{2,1,0:T(8,128)(2,1)} %param.19) | copy-start | bytes 98308
  102.7 153.1 %all-gather.2.cloned.1.call-start = ((), (), s32[]{:S(2)}) async-start(), calls=%async_computation.6 | async-start | bytes 6881280 | tf_op jit(solution)/shard_map/all_gather | solution.py:90
  152.4 2.0 copy-start.23
  255.8 5.4 copy-start.4
  255.8 5.4 copy-start.14
  261.2 1.8 copy-start.15
  266.7 7.2 %copy-start.13 = (bf16[1,192,1792]{2,1,0:T(8,128)(2,1)S(1)}, bf16[1,192,1792]{2,1,0:T(8,128)(2,1)}, u32[]{:S(2)}) copy-start(bf16[1,192,1792]{2,1,0:T(8,128)(2,1)} %param.35) | copy-start | bytes 2064388
  266.7 50.3 %all-to-all-start = ((f32[4,192,576]{2,1,0:T(8,128)}), f32[4,192,576]{2,1,0:T(8,128)}, u32[]{:S(2)}, u32[]{:S(2)}) async-start(f32[4,192,576]{2,1,0:T(8,128)} %bitcast.4), calls=%async_computation.2 | async-start | bytes 3932160 | tf_op jit(solution)/shard_map/all_to_all | solution.py:99
  271.3 5.3 copy-start.3
  271.3 5.3 copy-start.16
  271.3 139.7 %reduce-scatter.10.cloned.1.call-start = ((), (), s32[]{:S(2)}) async-start(), calls=%async_computation.7 | async-start | bytes 1769472
  322.9 2.5 copy-start.10
  331.8 15.0 %copy-start.5 = (f32[192,2,7,64]{3,2,1,0:T(8,128)S(1)}, f32[192,2,7,64]{3,2,1,0:T(8,128)}, u32[]{:S(2)}) copy-start(f32[192,2,7,64]{3,2,1,0:T(8,128)} %get-tuple-element.19) | copy-start | bytes 2064388
  346.9 3.4 copy-start.19
  360.9 7.1 %copy-start.6 = (bf16[192,2,7,128]{3,2,1,0:T(8,128)(2,1)S(1)}, bf16[192,2,7,128]{3,2,1,0:T(8,128)(2,1)}, u32[]{:S(2)}) copy-start(bf16[192,2,7,128]{3,2,1,0:T(8,128)(2,1)} %reshape_squeeze.3) | copy-start | bytes 2064388
  367.9 3.2 copy-start.2
  372.8 1.5 copy-start.20
  372.9 134.8 %all-reduce.8.cloned.1.call-start = ((), (), s32[]{:S(2)}) async-start(), calls=%async_computation.9 | async-start | bytes 4718592 | tf_op jit(solution)/shard_map/psum | solution.py:168
  372.9 15.1 %copy-start.7 = (bf16[192,2,7,128]{3,2,1,0:T(8,128)(2,1)S(1)}, bf16[192,2,7,128]{3,2,1,0:T(8,128)(2,1)}, u32[]{:S(2)}) copy-start(bf16[192,2,7,128]{3,2,1,0:T(8,128)(2,1)} %reshape_squeeze.3) | copy-start | bytes 2064388
  394.7 9.5 %copy-start.18 = (f32[192,64]{1,0:T(8,128)S(1)}, f32[192,64]{1,0:T(8,128)}, u32[]{:S(2)}) copy-start(f32[192,64]{1,0:T(8,128)} %get-tuple-element.23) | copy-start | bytes 147460
  406.9 2.3 copy-start.11
  414.3 93.4 %copy-start.8 = (bf16[192,2,7,128]{3,0,2,1:T(8,128)(2,1)S(1)}, bf16[192,2,7,128]{3,0,2,1:T(8,128)(2,1)}, u32[]{:S(2)}) copy-start(bf16[192,2,7,128]{3,0,2,1:T(8,128)(2,1)} %get-tuple-element.31) | copy-start | bytes 2064388
  414.3 159.2 %all-reduce.6.cloned.1.call-start = ((), (), s32[]{:S(2)}) async-start(), calls=%async_computation.8 | async-start | bytes 4718592 | tf_op jit(solution)/shard_map/psum | solution.py:167
  573.6 2.3 copy-start.17
  573.6 3.1 copy-start.12
  573.6 4.0 copy-start.21
  573.6 4.7 copy-start.1
Sparse Core Ops, SparseCore 0:
  30.0 51.8 reduce-scatter.5
  102.8 19.9 reduce-scatter.7
  156.1 99.6 all-gather.1
  373.0 36.4 reduce-scatter.9
  414.4 93.1 all-reduce.7
  511.1 62.3 all-reduce.5
